TPU v7x, 256 devices: a whole 4x4x8 slice. The times are simulated.
256 devices in a mesh: feeder: 64 (over z, x, core), node: 4 (over y).
Axes of the slice: x: 4, y: 4, z: 8, core: 2. Of those that a mesh axis runs over, the one named last changes fastest.
Arguments:
- factors: bfloat16 [2048, 256], P('node'), may hold values from -6 to 6
- loadings: bfloat16 [32768, 256], P(('feeder', 'node')), may hold values from -0.35355339 to 0.5
- parents: int32 [32768], P(('feeder', 'node')), may hold values from -1 to 126, as said below
- load_base: float32 [2, 32768], P(None, ('feeder', 'node')), may hold values from 2.4414063e-06 to 0.00048828125, as said below
- lateral_z: float32 [2, 32768], P(None, ('feeder', 'node')), may hold values from 0.007 to 0.175, as said below
- trunk_z: float32 [2, 64, 4], P(None, 'feeder', 'node'), may hold values from 0.00034375 to 0.00609375, as said below
Outputs:
- volt_real: float32 [2048, 32768], P(None, ('feeder', 'node'))
- volt_imag: float32 [2048, 32768], P(None, ('feeder', 'node'))
Inputs may be any that keep to these rules, and one draw needn't show every extreme that they name: `parents`: within each aligned run of 128 nodes (one lateral), a node's entry is the position of its parent in the same lateral, which comes before it, or -1 for a branch from the section's head node; the first node of every lateral has -1 and the last node's parent is the node just before it. `load_base`: with unit = 1 / 8192, row 0 lies between 1 and 4 units and row 1 between 0.02 and 0.08 units. `lateral_z`: with unit = 128 * 64 / 128^2, row 0 lies between 0.014 and 0.056 units and row 1 between 0.087 and 0.35 units. `trunk_z`: with unit = 1 / 64, row 0 lies between 0.022 and 0.066 units and row 1 between 0.13 and 0.39 units.
All inputs are finite; a program needn't handle non-finite values.
Results may differ from a plain program's by a relative error of at most 0.0003.
Values may be sent and summed in bfloat16 or wider, within the bound.
A program may use at most 64 MiB of HBM per device.

v0:
```python
import jax
import jax.numpy as jnp
from jax import lax
from jax.sharding import PartitionSpec as P

LAT_NODES = 128
SWEEPS = 3


HIGHEST = lax.Precision.HIGHEST


def carried_in(part, axis, combine, identity, reverse):
    count = lax.axis_size(axis)
    place = lax.axis_index(axis)
    ahead = count - 1 - place if reverse else place
    gathered = lax.all_gather(part, axis)
    state = jnp.zeros_like(part) + jnp.asarray(identity, part.dtype)

    def one(turn, state):
        source = count - 1 - turn if reverse else turn
        return combine(state, lax.dynamic_index_in_dim(gathered, source, 0, False))

    return lax.fori_loop(0, ahead, one, state)


def path_matrix(parent_rows):
    laterals, width = parent_rows.shape
    column = jnp.arange(width, dtype=jnp.int32)
    adjacency = (parent_rows[:, :, None] == column[None, None, :]).astype(jnp.float32)
    identity = jnp.eye(width, dtype=jnp.float32)
    paths = identity[None] + adjacency
    power = adjacency
    for turn in range((width - 1).bit_length() - 1):
        power = jnp.einsum("alm,amn->aln", power, power, precision=HIGHEST)
        paths = paths + jnp.einsum("alm,amn->aln", paths, power, precision=HIGHEST)
    return paths


def node_currents(active, reactive, real_part, imag_part):
    magnitude = real_part * real_part + imag_part * imag_part
    return (
        (active * real_part + reactive * imag_part) / magnitude,
        (active * imag_part - reactive * real_part) / magnitude,
    )


def add_total(earlier, later):
    return earlier + later


def lateral_products(stacked, tables):
    blocks = jnp.dot(stacked, tables[0], precision=HIGHEST, preferred_element_type=jnp.float32)
    return blocks


def trunk_heads(inject, trunk_z, scen):
    resist_trunk = trunk_z[0, 0, 0]
    react_trunk = trunk_z[1, 0, 0]
    zeros = jnp.zeros_like(inject)
    beyond = carried_in(inject, "feeder", add_total, zeros, True)
    trunk = inject + beyond
    trunk_real = trunk[:scen]
    trunk_imag = trunk[scen:]
    drop = jnp.concatenate(
        [
            resist_trunk * trunk_real - react_trunk * trunk_imag,
            resist_trunk * trunk_imag + react_trunk * trunk_real,
        ]
    )
    before = carried_in(drop, "feeder", add_total, zeros, False)
    total = before + drop
    return (1.0 - total[:scen], -total[scen:])


def local(factors, loadings, parents, load_base, lateral_z, trunk_z):
    levels = jnp.einsum(
        "sr,nr->sn",
        lax.all_gather(factors, "node", axis=0, tiled=True),
        loadings,
        preferred_element_type=jnp.float32,
    ).astype(jnp.bfloat16)
    scen = levels.shape[0]
    nodes_here = levels.shape[1]
    lat_count = nodes_here // LAT_NODES
    swing = 1.0 + 0.5 * jnp.tanh(levels.astype(jnp.float32))
    active = load_base[0][None, :] * swing
    reactive = load_base[1][None, :] * swing
    paths = path_matrix(parents.reshape(lat_count, LAT_NODES))
    paths_back = jnp.swapaxes(paths, 1, 2)
    resist = lateral_z[0][None, :]
    react = lateral_z[1][None, :]
    volts = jnp.concatenate(
        [jnp.ones((scen, nodes_here), jnp.float32), jnp.zeros((scen, nodes_here), jnp.float32)]
    )
    for sweep_index in range(SWEEPS):
        current_real, current_imag = node_currents(active, reactive, volts[:scen], volts[scen:])
        current = jnp.concatenate([current_real, current_imag])
        inject = jnp.sum(current, axis=1)
        branch = lateral_products(current, paths)
        branch_real = branch[:scen]
        branch_imag = branch[scen:]
        weighted = jnp.concatenate(
            [resist * branch_real - react * branch_imag, resist * branch_imag + react * branch_real]
        )
        drops = lateral_products(weighted, paths_back)
        head_real, head_imag = trunk_heads(inject, trunk_z, scen)
        volts = jnp.concatenate(
            [head_real[:, None] - drops[:scen], head_imag[:, None] - drops[scen:]]
        )
    return (volts[:scen], volts[scen:])


def solution(mesh):
    return jax.shard_map(
        local,
        mesh=mesh,
        in_specs=(
            P("node", None),
            P(("feeder", "node"), None),
            P(("feeder", "node")),
            P(None, ("feeder", "node")),
            P(None, ("feeder", "node")),
            P(None, "feeder", "node"),
        ),
        out_specs=(P(None, ("feeder", "node")), P(None, ("feeder", "node"))),
        check_vma=False,
    )
```

profile of v0, /device:TPU:1, one launch (start us, length us, event | category | flops | bytes accessed | tf_op | source)
XLA Modules:
  0.0 646.7 jit_solution(12022927235953794426)
XLA Ops:
  8.7 29.5 %all-gather.14.cloned.1.call-done = bf16[2048,256]{1,0:T(8,128)(2,1)} async-done(((bf16[512,256]{1,0:T(8,128)(2,1)}), bf16[2048,256]{1,0:T(8,128)(2,1)}) %all-gather.14.cloned.1.call-update) | async-done | bytes 1048592 | tf_op jit(solution)/shard_map/all_gather | solution.py:79
  38.2 1.7 multiply_add_fusion.5
  43.6 77.6 %all-gather.16.cloned.1.call-done = f32[262144]{0:T(1024)} async-done(((f32[4096]{0:T(1024)}), f32[262144]{0:T(1024)}) %all-gather.16.cloned.1.call-update) | async-done | bytes 1048592 | tf_op jit(solution)/shard_map/all_gather | solution.py:17
  121.2 2.4 reshape.172
  123.6 59.7 %while.66 = (s32[]{:T(128)}, f32[4096]{0:T(1024)S(1)}, s32[]{:T(128)}, f32[64,4096]{1,0:T(8,128)}, s32[]{:T(128)}, /*index=5*/s32[]{:T(128)}, s32[]{:T(128)}, s32[]{:T(128)}) while((s32[]{:T(128)}, f32[4096]{0:T(1024)S(1)}, s32[]{:T(128)}, f32[64,4096]{1,0:T(8,128)}, s32[]{:T(128)}, /*index=5*/s32[]{:T(128)}, s32[]{:T(128)}, s32[]{:T(128)}) %tuple.128), condition=%wide.region_2.3_spmd, body=%wide.region_1.2_spmd.sunk | while | flops 4102 | bytes 82055 | solution.py:24
  186.0 1.9 fusion.20
  188.2 3.2 fusion.4
  191.3 65.4 %all-gather.18.cloned.1.call-done = f32[262144]{0:T(1024)} async-done(((f32[4096]{0:T(1024)}), f32[262144]{0:T(1024)}) %all-gather.18.cloned.1.call-update) | async-done | bytes 1048592 | tf_op jit(solution)/shard_map/all_gather | solution.py:17
  256.7 1.4 reshape.173
  258.2 2.0 fusion.23
  261.5 77.3 %all-gather.20.cloned.1.call-done = f32[262144]{0:T(1024)} async-done(((f32[4096]{0:T(1024)}), f32[262144]{0:T(1024)}) %all-gather.20.cloned.1.call-update) | async-done | bytes 1048592 | tf_op jit(solution)/shard_map/all_gather | solution.py:17
  338.8 2.4 reshape.174
  341.2 59.7 %while.68 = (s32[]{:T(128)}, f32[4096]{0:T(1024)S(1)}, s32[]{:T(128)}, f32[64,4096]{1,0:T(8,128)}, s32[]{:T(128)}, /*index=5*/s32[]{:T(128)}, s32[]{:T(128)}, s32[]{:T(128)}) while((s32[]{:T(128)}, f32[4096]{0:T(1024)S(1)}, s32[]{:T(128)}, f32[64,4096]{1,0:T(8,128)}, s32[]{:T(128)}, /*index=5*/s32[]{:T(128)}, s32[]{:T(128)}, s32[]{:T(128)}) %tuple.134), condition=%wide.region_7.8_spmd, body=%wide.region_6.7_spmd.sunk | while | flops 4102 | bytes 82055 | solution.py:24
  403.0 1.9 fusion.18
  405.1 3.2 fusion.8
  408.3 66.1 %all-gather.22.cloned.1.call-done = f32[262144]{0:T(1024)} async-done(((f32[4096]{0:T(1024)}), f32[262144]{0:T(1024)}) %all-gather.22.cloned.1.call-update) | async-done | bytes 1048592 | tf_op jit(solution)/shard_map/all_gather | solution.py:17
  475.9 2.0 fusion.22
  479.2 77.3 %all-gather.24.cloned.1.call-done = f32[262144]{0:T(1024)} async-done(((f32[4096]{0:T(1024)}), f32[262144]{0:T(1024)}) %all-gather.24.cloned.1.call-update) | async-done | bytes 1048592 | tf_op jit(solution)/shard_map/all_gather | solution.py:17
  557.9 4.0 while.70
  563.8 1.9 fusion.16
  565.9 1.8 fusion.12
  567.7 68.9 %all-gather.26.cloned.1.call-done = f32[262144]{0:T(1024)} async-done(((f32[4096]{0:T(1024)}), f32[262144]{0:T(1024)}) %all-gather.26.cloned.1.call-update) | async-done | bytes 1048592 | tf_op jit(solution)/shard_map/all_gather | solution.py:17
  636.6 1.4 reshape.177
  638.2 1.7 slice_subtract_fusion
  (453 shorter events, 134.7 us)
Async XLA Ops:
  7.2 31.1 %copy-start = (bf16[128,256]{1,0:T(8,128)(2,1)S(1)}, bf16[128,256]{1,0:T(8,128)(2,1)}, u32[]{:S(2)}) copy-start(bf16[128,256]{1,0:T(8,128)(2,1)} %param.19) | copy-start | bytes 196612
  7.2 31.0 %all-gather.14.cloned.1.call-start = ((), (), s32[]{:S(2)}) async-start(), calls=%async_computation | async-start | bytes 1310720 | tf_op jit(solution)/shard_map/all_gather | solution.py:79
  7.9 113.3 %all-gather.16.cloned.1.call-start = ((), (), s32[]{:S(2)}) async-start(), calls=%async_computation.1 | async-start | bytes 1064960 | tf_op jit(solution)/shard_map/all_gather | solution.py:17
  40.0 1.3 copy-start.5
  40.0 1.9 copy-start.4
  41.2 142.0 %copy-start.1 = (f32[4096]{0:T(1024)S(1)}, f32[4096]{0:T(1024)}, u32[]{:S(2)}) copy-start(f32[4096]{0:T(1024)} %fusion.21) | copy-start | bytes 49156
  41.2 215.4 %all-gather.18.cloned.1.call-start = ((), (), s32[]{:S(2)}) async-start(), calls=%async_computation.2 | async-start | bytes 1064960 | tf_op jit(solution)/shard_map/all_gather | solution.py:17
  42.1 143.1 %copy-start.6 = (f32[2,128]{1,0:T(2,128)S(1)}, f32[2,128]{1,0:T(2,128)}, u32[]{:S(2)}) copy-start(f32[2,128]{1,0:T(2,128)} %param.22) | copy-start | bytes 3076
  185.1 153.7 %all-gather.20.cloned.1.call-start = ((), (), s32[]{:S(2)}) async-start(), calls=%async_computation.3 | async-start | bytes 1064960 | tf_op jit(solution)/shard_map/all_gather | solution.py:17
  261.4 139.5 %copy-start.3 = (f32[4096]{0:T(1024)S(1)}, f32[4096]{0:T(1024)}, u32[]{:S(2)}) copy-start(f32[4096]{0:T(1024)} %fusion.19) | copy-start | bytes 49156
  261.4 212.9 %all-gather.22.cloned.1.call-start = ((), (), s32[]{:S(2)}) async-start(), calls=%async_computation.4 | async-start | bytes 1064960 | tf_op jit(solution)/shard_map/all_gather | solution.py:17
  402.8 153.7 %all-gather.24.cloned.1.call-start = ((), (), s32[]{:S(2)}) async-start(), calls=%async_computation.5 | async-start | bytes 1064960 | tf_op jit(solution)/shard_map/all_gather | solution.py:17
  479.1 82.9 %copy-start.2 = (f32[4096]{0:T(1024)S(1)}, f32[4096]{0:T(1024)}, u32[]{:S(2)}) copy-start(f32[4096]{0:T(1024)} %fusion.17) | copy-start | bytes 49156
  479.1 157.5 %all-gather.26.cloned.1.call-start = ((), (), s32[]{:S(2)}) async-start(), calls=%async_computation.6 | async-start | bytes 1064960 | tf_op jit(solution)/shard_map/all_gather | solution.py:17
Sparse Core Ops, SparseCore 0:
  9.8 28.3 all-gather.13
  41.6 79.5 all-gather.15
  185.2 71.4 all-gather.17
  261.6 77.2 all-gather.19
  402.9 71.4 all-gather.21
  479.2 77.2 all-gather.23
  563.9 72.6 all-gather.25
where the time goes:
time: 649 us; the launch traced here: 647 us
  waiting for transfers between devices  463 us (71%)
  local copies, waits for them, and re-layouts  127 us (20%)
  matrix products  18 us (3%)
  other arithmetic  16.4 us (3%)
  between operations  14.6 us (2%)
  loops' own time  6.86 us (1%)
    all_gather x6, waiting for transfers between devices, carried_in(): gathered = lax.all_gather(part, axis)  433 us
    dynamic_slice x189, local copies, waits for them, and re-layouts, one(): return combine(state, lax.dynamic_index_in_dim(gathered, source, 0, False))  116 us
    all_gather x1, waiting for transfers between devices, local(): lax.all_gather(factors, 'node', axis=0, tiled=True)  29.5 us
    dot_general x6, matrix products, lateral_products(): jnp.dot(stacked, tables[0], precision=HIGHEST, preferred_element_type=jnp...  13.8 us
  transfers between devices with their start and end apart: 7, of which 7 were waited for; matrix products, arithmetic and copies ran while one was open for 3% of the time, Pallas kernels for 0%

commit v1 on v0

v1 whole, which is shorter than its diff:
```python
import functools

import jax
import jax.numpy as jnp
from jax import lax
from jax.experimental import pallas as pl
from jax.experimental.pallas import tpu as pltpu
from jax.sharding import PartitionSpec as P

MESH = pl.DeviceIdType.MESH
F32 = jnp.float32
BF16 = jnp.bfloat16
SWEEPS = 3
LANES = 128
PASS = 4


def dot(a, b, dims=((1,), (0,))):
    return lax.dot_general(a, b, (dims, ((), ())), preferred_element_type=F32)


def halves(value):
    high = value.astype(BF16)
    return high, (value - high.astype(F32)).astype(BF16)


def turn(tile):
    return pltpu.roll(tile, 4, 0)


def cmul(ratio, tile):
    return ratio[0] * tile + ratio[1] * turn(tile)


def body(
    slabs, slab, nodes, fac_ref, load_ref, par_ref, base_ref, latz_ref, trz_ref, out_r, out_i,
    fac, swing, cur, drop, dropl, wide, wlow, wlast, pcol, qcol, one_sec, two_sec, two_src, two_own,
    zsec, zlow, zmin, ztot, zpre, prep,
    load_v, par_v, base_v, latz_v,
    local_sem, fac_send, fac_recv, pair_send, pair_recv, zs_send, zs_recv, zt_send, zt_recv,
    one_send, one_recv, two_send, two_recv,
):
    feeder = lax.axis_index("feeder")
    node = lax.axis_index("node")
    zz = feeder // slab
    ss = lax.rem(feeder, slab)
    core = lax.rem(feeder, 2)
    partner = feeder + 1 - 2 * core
    chunk = fac.shape[1]
    half = chunk // 2
    offsets = [0, 1, nodes - 1] + [o for o in range(2, nodes - 1)]

    def slab_mate(turn_):
        return lax.rem(ss + turn_, slab)

    def at_slab(mate):
        return {"feeder": zz * slab + mate, "node": node}

    def at_other(other):
        return {"feeder": other * slab + ss, "node": node}

    def at_node(offset):
        return {"feeder": feeder, "node": lax.rem(node + offset, nodes)}

    far = sorted(range(1, slabs), key=lambda d: -min(d, slabs - d))
    wide_turns = sorted(range(1, slab), key=lambda d: -min(d, slab - d))

    barrier = pltpu.get_barrier_semaphore()
    greeted = 0
    for d in far:
        pl.semaphore_signal(barrier, inc=1, device_id=at_other(lax.rem(zz + d, slabs)), device_id_type=MESH)
        greeted += 1
    for d in wide_turns:
        pl.semaphore_signal(barrier, inc=1, device_id=at_slab(slab_mate(d)), device_id_type=MESH)
        greeted += 1
    for o in offsets[1:]:
        pl.semaphore_signal(barrier, inc=1, device_id=at_node(o), device_id_type=MESH)
        greeted += 1

    copies = [
        pltpu.make_async_copy(fac_ref, fac.at[0], local_sem.at[0]),
        pltpu.make_async_copy(load_ref, load_v, local_sem.at[1]),
        pltpu.make_async_copy(base_ref, base_v, local_sem.at[2]),
        pltpu.make_async_copy(par_ref, par_v, local_sem.at[3]),
        pltpu.make_async_copy(latz_ref, latz_v, local_sem.at[4]),
    ]
    for copy in copies:
        copy.start()
    for copy in copies:
        copy.wait()

    pcol[...] = jnp.broadcast_to(base_v[0:1, :], (LANES, LANES)).T
    qcol[...] = jnp.broadcast_to(base_v[1:2, :], (LANES, LANES)).T
    row8 = lax.broadcasted_iota(jnp.int32, (8, LANES), 0)
    upper = row8 < 4
    z_real = trz_ref[0]
    z_imag = trz_ref[1]
    zsec[ss, 0] = jnp.zeros((8, LANES), F32) + z_real
    zsec[ss, 1] = jnp.where(upper, -z_imag, z_imag)

    def level(c):
        for q in range(PASS):
            lo = q * LANES
            lev = dot(load_v[...], fac[c, lo:lo + LANES, :], ((1,), (1,)))
            swing[c, :, lo:lo + LANES] = 1.0 + 0.5 * jnp.tanh(lev.astype(BF16).astype(F32))

    rows = 16

    def currents(k, c, head):
        for q in range(PASS):
            lo = q * LANES
            if k:
                head_r = jnp.broadcast_to(head[q:q + 1, :], (rows, LANES))
                head_i = jnp.broadcast_to(head[q + 4:q + 5, :], (rows, LANES))

            def step(i, sums):
                at = pl.multiple_of(i * rows, rows)
                sw = swing[c, pl.ds(at, rows), lo:lo + LANES]
                p = pcol[pl.ds(at, rows), :]
                r = qcol[pl.ds(at, rows), :]
                if k:
                    vr = head_r - drop[c, pl.ds(at, rows), lo:lo + LANES]
                    vi = head_i - drop[c, pl.ds(LANES + at, rows), lo:lo + LANES]
                    t = sw / (vr * vr + vi * vi)
                    cr = t * (p * vr + r * vi)
                    ci = t * (p * vi - r * vr)
                else:
                    cr = sw * p
                    ci = -(sw * r)
                for part, value in ((0, cr), (1, ci)):
                    high, low = halves(value)
                    cur[c, pl.ds(part * LANES + at, rows), lo:lo + LANES] = high
                    cur[c, pl.ds((part + 2) * LANES + at, rows), lo:lo + LANES] = low
                return (
                    sums[0] + cr[0:8] + cr[8:16],
                    sums[1] + ci[0:8] + ci[8:16],
                )

            zero = jnp.zeros((8, LANES), F32)
            sum_r, sum_i = lax.fori_loop(0, LANES // rows, step, (zero, zero), unroll=4)
            one_sec[k, c, ss, q:q + 1, :] = jnp.sum(sum_r, axis=0, keepdims=True)
            one_sec[k, c, ss, q + 4:q + 5, :] = jnp.sum(sum_i, axis=0, keepdims=True)

    def send_one(k, c):
        for d in wide_turns:
            mate = slab_mate(d)
            pltpu.make_async_remote_copy(
                src_ref=one_sec.at[k, c, ss], dst_ref=one_sec.at[k, c, ss],
                send_sem=one_send.at[k, c], recv_sem=one_recv.at[k, c],
                device_id=at_slab(mate), device_id_type=MESH,
            ).start()

    def wait_bytes(sem, block):
        pltpu.make_async_copy(block, block, sem).wait()

    def combine(k, c):
        wait_bytes(one_recv.at[k, c], one_sec.at[k, c, pl.ds(0, slab - 1)])
        total = jnp.zeros((8, LANES), F32)
        weighted = total
        own = total
        for s in range(slab):
            tile = one_sec[k, c, s]
            swapped = turn(tile)
            total += tile
            weighted += zlow[s, 0] * tile + zlow[s, 1] * swapped
            own += zmin[s, 0] * tile + zmin[s, 1] * swapped
        if k:
            shift = cmul((zpre[zz, 0], zpre[zz, 1]), total)
            weighted += shift
            own += shift
        two_src[k, c, 0] = total
        two_src[k, c, 1] = weighted
        two_own[k, c, 0] = total
        two_own[k, c, 1] = own
        for d in far:
            other = lax.rem(zz + d, slabs)
            if k:
                later = (other > zz).astype(jnp.int32)
                source = two_src.at[k, c, pl.ds(later, 1)]
                target = two_sec.at[k, c, zz, pl.ds(0, 1)]
            else:
                source = two_src.at[k, c]
                target = two_sec.at[k, c, zz]
            pltpu.make_async_remote_copy(
                src_ref=source, dst_ref=target,
                send_sem=two_send.at[k, c], recv_sem=two_recv.at[k, c],
                device_id=at_other(other), device_id_type=MESH,
            ).start()

    def tiles(k, c, count):
        if k:
            return two_sec.at[k, c, pl.ds(0, count), pl.ds(0, 1)]
        return two_sec.at[k, c, pl.ds(0, count)]

    def heads(k, c):
        wait_bytes(two_recv.at[k, c], tiles(k, c, slabs - 1))
        near = two_own[k, c, 1]
        beyond = jnp.zeros((8, LANES), F32)
        if not k:
            near += cmul((zpre[zz, 0], zpre[zz, 1]), two_own[k, c, 0])
        for z in range(slabs):
            tile = two_sec[k, c, z, 0]
            beyond += jnp.where(z > zz, tile, 0.0)
            if k:
                near += jnp.where(z < zz, tile, 0.0)
            else:
                given = cmul((zpre[z, 0], zpre[z, 1]), tile) + two_sec[k, c, z, 1]
                near += jnp.where(z < zz, given, 0.0)
        here = (zpre[zz, 0] + zlow[ss, 0], zpre[zz, 1] + zlow[ss, 1])
        return jnp.where(upper, 1.0, 0.0) - near - cmul(here, beyond)

    def products(k, c):
        if k < SWEEPS - 1:
            drop[c] = dot(wide[...], cur[c]) + dot(wlow[...], cur[c, 0:2 * LANES, :])
        else:
            dropl[c] = dot(cur[c], wlast[0:4 * LANES, :], ((0,), (0,))) + dot(
                cur[c, 0:2 * LANES, :], wlast[4 * LANES:6 * LANES, :], ((0,), (0,))
            )

    def sweep(k, c):
        currents(k, c, heads(k - 1, c) if k else None)
        send_one(k, c)
        products(k, c)

    def finish(c):
        head = heads(SWEEPS - 1, c).T
        at = lax.rem(node + offsets[c], nodes) * chunk
        for q in range(PASS):
            where = pl.ds(pl.multiple_of(at + q * LANES, LANES), LANES)
            lo = q * LANES
            out_r[where, :] = head[:, q:q + 1] - dropl[c, lo:lo + LANES, 0:LANES]
            out_i[where, :] = head[:, q + 4:q + 5] - dropl[c, lo:lo + LANES, LANES:2 * LANES]

    mine = pl.ds(pl.multiple_of(core * half, half), half)

    def give(c):
        return pltpu.make_async_remote_copy(
            src_ref=fac.at[0, mine], dst_ref=fac.at[c, mine],
            send_sem=fac_send.at[c], recv_sem=fac_recv.at[c],
            device_id=at_node(nodes - offsets[c]), device_id_type=MESH,
        )

    def pass_on(c):
        return pltpu.make_async_remote_copy(
            src_ref=fac.at[c, mine], dst_ref=fac.at[c, mine],
            send_sem=pair_send.at[c], recv_sem=pair_recv.at[c],
            device_id={"feeder": partner, "node": node}, device_id_type=MESH,
        )

    level(0)
    currents(0, 0, None)
    pl.semaphore_wait(barrier, greeted)
    for d in wide_turns:
        pltpu.make_async_remote_copy(
            src_ref=zsec.at[ss], dst_ref=zsec.at[ss], send_sem=zs_send, recv_sem=zs_recv,
            device_id=at_slab(slab_mate(d)), device_id_type=MESH,
        ).start()
    send_one(0, 0)
    for c in range(1, nodes):
        give(c).start()

    width = LANES
    down = lax.broadcasted_iota(jnp.int32, (width, width), 0)
    across = lax.broadcasted_iota(jnp.int32, (width, width), 1)
    adjacent = jnp.where(jnp.broadcast_to(par_v[...], (width, width)) == down, 1.0, 0.0).T
    paths = jnp.where(down == across, 1.0, 0.0) + adjacent
    power = adjacent.astype(BF16)
    for turn_ in range((width - 1).bit_length() - 1):
        power = dot(power, power).astype(BF16)
        paths = paths + dot(paths.astype(BF16), power)
    paths_low = paths.astype(BF16)
    for part in range(2):
        z_row = jnp.broadcast_to(latz_v[part:part + 1, :], (width, width))
        z_high, z_mid = halves(z_row)
        z_low = (z_row - z_high.astype(F32) - z_mid.astype(F32)).astype(BF16)
        table = jnp.zeros((width, width), F32)
        for piece in (z_low, z_mid, z_high):
            table += dot((paths * piece.astype(F32)).astype(BF16), paths_low, ((1,), (1,)))
        prep[part] = table
    for part, sign, r0, c0 in ((0, 1.0, 0, 0), (1, -1.0, 0, 1), (1, 1.0, 1, 0), (0, 1.0, 1, 1)):
        high, low = halves(prep[part] * sign)
        rs, cs = slice(r0 * width, (r0 + 1) * width), slice(c0 * width, (c0 + 1) * width)
        wide[rs, cs] = high
        wide[rs, (c0 + 2) * width:(c0 + 3) * width] = high
        wlow[rs, cs] = low
        ts, us = slice(c0 * width, (c0 + 1) * width), slice(r0 * width, (r0 + 1) * width)
        wlast[ts, us] = high
        wlast[(c0 + 2) * width:(c0 + 3) * width, us] = high
        wlast[(c0 + 4) * width:(c0 + 5) * width, us] = low

    wait_bytes(zs_recv, zsec.at[pl.ds(0, slab - 1)])
    run_r = jnp.zeros((8, LANES), F32)
    run_i = run_r
    cut_r = run_r
    cut_i = run_r
    for s in range(slab):
        run_r += zsec[s, 0]
        run_i += zsec[s, 1]
        cut_r += jnp.where(s <= ss, zsec[s, 0], 0.0)
        cut_i += jnp.where(s <= ss, zsec[s, 1], 0.0)
        zlow[s, 0] = run_r
        zlow[s, 1] = run_i
        zmin[s, 0] = cut_r
        zmin[s, 1] = cut_i
    ztot[zz, 0] = run_r
    ztot[zz, 1] = run_i
    for d in far:
        pltpu.make_async_remote_copy(
            src_ref=ztot.at[zz], dst_ref=ztot.at[zz], send_sem=zt_send, recv_sem=zt_recv,
            device_id=at_other(lax.rem(zz + d, slabs)), device_id_type=MESH,
        ).start()
    combine(0, 0)
    products(0, 0)

    def bring(c):
        give(c).wait_recv()
        pass_on(c).start()

    def begin(c):
        pass_on(c).wait_recv()
        level(c)
        sweep(0, c)

    bring(1)
    if nodes > 2:
        bring(2)
    begin(1)
    if nodes > 2:
        begin(2)
    combine(0, 1)
    if nodes > 2:
        combine(0, 2)
    for c in range(3, nodes):
        bring(c)
        begin(c)

    wait_bytes(zt_recv, ztot.at[pl.ds(0, slabs - 1)])
    run_r = jnp.zeros((8, LANES), F32)
    run_i = run_r
    for z in range(slabs):
        zpre[z, 0] = run_r
        zpre[z, 1] = run_i
        run_r += ztot[z, 0]
        run_i += ztot[z, 1]

    for k in range(1, SWEEPS + 1):
        last = k == SWEEPS
        step = finish if last else functools.partial(sweep, k)
        step(0)
        for c in range(3, nodes):
            combine(k - 1, c)
        if not last:
            combine(k, 0)
        step(1)
        if nodes > 2:
            step(2)
        if not last:
            combine(k, 1)
            if nodes > 2:
                combine(k, 2)
        for c in range(3, nodes):
            step(c)

    wait_bytes(zs_send, zsec.at[pl.ds(0, slab - 1)])
    wait_bytes(zt_send, ztot.at[pl.ds(0, slabs - 1)])
    for c in range(1, nodes):
        give(c).wait_send()
        pass_on(c).wait_send()
    for k in range(SWEEPS):
        for c in range(nodes):
            wait_bytes(one_send.at[k, c], one_sec.at[k, c, pl.ds(0, slab - 1)])
            wait_bytes(two_send.at[k, c], tiles(k, c, slabs - 1))


def local(slabs, slab, nodes, factors, loadings, parents, load_base, lateral_z, trunk_z):
    chunk, depth = factors.shape
    scen = chunk * nodes
    width = loadings.shape[0]
    any_space = pl.BlockSpec(memory_space=pl.ANY)
    dma = pltpu.SemaphoreType.DMA
    out = jax.ShapeDtypeStruct((scen, width), F32)
    tile = (8, LANES)
    return pl.pallas_call(
        functools.partial(body, slabs, slab, nodes),
        out_shape=(out, out),
        in_specs=[any_space] * 5 + [pl.BlockSpec(memory_space=pltpu.SMEM)],
        out_specs=(pl.BlockSpec(memory_space=pltpu.VMEM),) * 2,
        scratch_shapes=[
            pltpu.VMEM((nodes, chunk, depth), BF16),
            pltpu.VMEM((nodes, width, chunk), F32),
            pltpu.VMEM((nodes, 4 * width, chunk), BF16),
            pltpu.VMEM((nodes, 2 * width, chunk), F32),
            pltpu.VMEM((nodes, chunk, 2 * width), F32),
            pltpu.VMEM((2 * width, 4 * width), BF16),
            pltpu.VMEM((2 * width, 2 * width), BF16),
            pltpu.VMEM((6 * width, 2 * width), BF16),
            pltpu.VMEM((width, LANES), F32),
            pltpu.VMEM((width, LANES), F32),
            pltpu.VMEM((SWEEPS, nodes, slab) + tile, F32),
            pltpu.VMEM((SWEEPS, nodes, slabs, 2) + tile, F32),
            pltpu.VMEM((SWEEPS, nodes, 2) + tile, F32),
            pltpu.VMEM((SWEEPS, nodes, 2) + tile, F32),
            pltpu.VMEM((slab, 2) + tile, F32),
            pltpu.VMEM((slab, 2) + tile, F32),
            pltpu.VMEM((slab, 2) + tile, F32),
            pltpu.VMEM((slabs, 2) + tile, F32),
            pltpu.VMEM((slabs, 2) + tile, F32),
            pltpu.VMEM((2, width, width), F32),
            pltpu.VMEM((width, depth), BF16),
            pltpu.VMEM((1, width), jnp.int32),
            pltpu.VMEM((2, width), F32),
            pltpu.VMEM((2, width), F32),
            dma((5,)),
            dma((nodes,)),
            dma((nodes,)),
            dma((nodes,)),
            dma((nodes,)),
            dma(()),
            dma(()),
            dma(()),
            dma(()),
            dma((SWEEPS, nodes)),
            dma((SWEEPS, nodes)),
            dma((SWEEPS, nodes)),
            dma((SWEEPS, nodes)),
        ],
        compiler_params=pltpu.CompilerParams(
            collective_id=0, has_side_effects=True, vmem_limit_bytes=48 * 1024 * 1024
        ),
    )(factors, loadings, parents.reshape(1, width), load_base, lateral_z, trunk_z.reshape(2))


def solution(mesh):
    feeder = mesh.shape["feeder"]
    slab = 8 if feeder >= 64 else 2
    return jax.shard_map(
        functools.partial(local, feeder // slab, slab, mesh.shape["node"]),
        mesh=mesh,
        in_specs=(
            P("node", None),
            P(("feeder", "node"), None),
            P(("feeder", "node")),
            P(None, ("feeder", "node")),
            P(None, ("feeder", "node")),
            P(None, "feeder", "node"),
        ),
        out_specs=(P(None, ("feeder", "node")), P(None, ("feeder", "node"))),
        check_vma=False,
    )
```

time: 649 us -> 54.8 us (0.08)
  waiting for transfers between devices: 463 us -> 0 us
  local copies, waits for them, and re-layouts: 127 us -> 4.41 us
  Pallas kernels: 0 us -> 49.5 us
  matrix products: 18 us -> 0 us
  other arithmetic: 16.4 us -> 0 us
  between operations: 14.6 us -> 0.68 us
  loops' own time: 6.86 us -> 0 us
    all_gather x7 -> x0, waiting for transfers between devices: 462 us -> none  [the longest x6 433 us: carried_in(): gathered = lax.all_gather(part, axis)]
    dynamic_slice x189 -> x0, local copies, waits for them, and re-layouts: 116 us -> none  [one(): return combine(state, lax.dynamic_index_in_dim(gathered, source, 0, False))]
    pallas_call x0 -> x1, Pallas kernels: none -> 49.5 us  [local(): pl.pallas_call(functools.partial(body, slabs, slab, nodes), out_shape=(ou...]
    dot_general x19 -> x0, matrix products: 18 us -> none  [the longest x6 13.8 us: lateral_products(): jnp.dot(stacked, tables[0], precision=HIGHEST, preferred_element_type=jnp...]
    all_gather x6 -> x0, local copies, waits for them, and re-layouts: 10.4 us -> none  [carried_in(): gathered = lax.all_gather(part, axis)]
    another operation x6 -> x0, loops' own time: 6.86 us -> none  [carried_in(): return lax.fori_loop(0, ahead, one, state)]
  transfers between devices with their start and end apart: 7 -> 0, of which waited for: 7 -> 0; matrix products, arithmetic and copies ran while one was open for 3% -> 0% of each run, Pallas kernels for 0% -> 0%
where the time goes in v1:
time: 54.8 us; the launch traced here: 54.6 us
  Pallas kernels  49.5 us (90%)
  local copies, waits for them, and re-layouts  4.41 us (8%)
  between operations  0.68 us (1%)
    pallas_call x1, Pallas kernels, local(): pl.pallas_call(functools.partial(body, slabs, slab, nodes), out_shape=(ou...  49.5 us
    unnamed x14, local copies, waits for them, and re-layouts  4.41 us

profile of v1, /device:TPU:1, one launch (start us, length us, event | category | flops | bytes accessed | tf_op | source)
XLA Modules:
  0.0 54.6 jit_solution(14877626191815572367)
XLA Ops:
  0.6 0.0 copy-start.3
  0.6 0.0 copy-start.5
  0.7 0.0 copy-start.2
  0.7 0.0 copy-start.4
  0.7 0.6 %copy-done.3 = f32[2,128]{1,0:T(2,128)S(1)} copy-done((f32[2,128]{1,0:T(2,128)S(1)}, f32[2,128]{1,0:T(2,128)}, u32[]{:S(2)}) %copy-start.3) | copy-done | bytes 1048
  1.3 0.0 copy-done.5
  1.3 0.0 copy-done.2
  1.3 0.0 copy-done.4
  1.3 0.0 copy-start
  1.3 0.9 %copy-done = bf16[512,256]{1,0:T(8,128)(2,1)S(1)} copy-done((bf16[512,256]{1,0:T(8,128)(2,1)S(1)}, bf16[512,256]{1,0:T(8,128)(2,1)}, u32[]{:S(2)}) %copy-start) | copy-done | bytes 262168
  2.3 0.0 copy-start.1
  2.3 0.8 %copy-done.1 = bf16[128,256]{1,0:T(8,128)(2,1)S(1)} copy-done((bf16[128,256]{1,0:T(8,128)(2,1)S(1)}, bf16[128,256]{1,0:T(8,128)(2,1)}, u32[]{:S(2)}) %copy-start.1) | copy-done | bytes 65560
  3.1 49.5 %shard_map.77 = (f32[2048,128]{1,0:T(8,128)S(1)}, f32[2048,128]{1,0:T(8,128)S(1)}) custom-call(bf16[512,256]{1,0:T(8,128)(2,1)S(1)} %copy-done, bf16[128,256]{1,0:T(8,128)(2,1)S(1)} %copy-done.1, s32[1,128]{1,0:T(1,128)S(1)} %bitcast.2, f32[2,128]{1,0:T(2,128)S(1)} %copy-done.2, f32[2,128]{1,0:T(2,128)S(1)} %copy-done.3, f32[2]{0:T(128)S(1)} %bitcast.3), custom_call_target="tpu_custom_call" | custom-call | tf_op jit(solution)/shard_map/pallas_call | solution.py:383
  52.7 1.0 %copy.10 = f32[2048,128]{1,0:T(8,128)} copy(f32[2048,128]{1,0:T(8,128)S(1)} %get-tuple-element.4) | data formatting | bytes 2097152
  53.6 1.0 %copy.11 = f32[2048,128]{1,0:T(8,128)} copy(f32[2048,128]{1,0:T(8,128)S(1)} %get-tuple-element.5) | data formatting | bytes 2097152
Async XLA Ops:
  0.6 0.7 %copy-start.3 = (f32[2,128]{1,0:T(2,128)S(1)}, f32[2,128]{1,0:T(2,128)}, u32[]{:S(2)}) copy-start(f32[2,128]{1,0:T(2,128)} %latz_ref.1) | copy-start | bytes 3076
  0.6 0.7 %copy-start.5 = (f32[2,1,1]{0,2,1:T(1,128)S(1)}, f32[2,1,1]{0,2,1:T(1,128)}, u32[]{:S(2)}) copy-start(f32[2,1,1]{0,2,1:T(1,128)} %param.11) | copy-start | bytes 28
  0.7 0.7 %copy-start.2 = (f32[2,128]{1,0:T(2,128)S(1)}, f32[2,128]{1,0:T(2,128)}, u32[]{:S(2)}) copy-start(f32[2,128]{1,0:T(2,128)} %base_ref.1) | copy-start | bytes 3076
  0.7 0.7 %copy-start.4 = (s32[128]{0:T(128)S(1)}, s32[128]{0:T(128)}, u32[]{:S(2)}) copy-start(s32[128]{0:T(128)} %param.8) | copy-start | bytes 1540
  1.3 1.0 %copy-start = (bf16[512,256]{1,0:T(8,128)(2,1)S(1)}, bf16[512,256]{1,0:T(8,128)(2,1)}, u32[]{:S(2)}) copy-start(bf16[512,256]{1,0:T(8,128)(2,1)} %fac_ref.1) | copy-start | bytes 786436
  2.3 0.8 %copy-start.1 = (bf16[128,256]{1,0:T(8,128)(2,1)S(1)}, bf16[128,256]{1,0:T(8,128)(2,1)}, u32[]{:S(2)}) copy-start(bf16[128,256]{1,0:T(8,128)(2,1)} %load_ref.1) | copy-start | bytes 196612

commit v2 on v1

--- a/solution.py
+++ b/solution.py
@@ -12,6 +12,27 @@
 BF16 = jnp.bfloat16
 SWEEPS = 3
 LANES = 128
+ORDER = (
+    "L0 C00 X P",
+    "S B00",
+    "G1 G2",
+    "L1 A01",
+    "L2 A02",
+    "G3 M00 M01",
+    "L3 A03",
+    "M02 M03",
+    "Z A10 B01",
+    "B02 B03 M10 B10",
+    "A11 A12 A13",
+    "M11 M12 M13",
+    "A20 B11 B12 B13",
+    "M20 B20",
+    "A21 A22 A23",
+    "M21 M22 M23",
+    "F0 B21 B22 B23",
+    "F1 F2 F3",
+)
+PIECES = 4
 PASS = 4
 
 
@@ -36,7 +57,7 @@
     slabs, slab, nodes, fac_ref, load_ref, par_ref, base_ref, latz_ref, trz_ref, out_r, out_i,
     fac, swing, cur, drop, dropl, wide, wlow, wlast, pcol, qcol, one_sec, two_sec, two_src, two_own,
     zsec, zlow, zmin, ztot, zpre, prep,
-    load_v, par_v, base_v, latz_v,
+    load_v, par_v, base_v, latz_v, trz_s,
     local_sem, fac_send, fac_recv, pair_send, pair_recv, zs_send, zs_recv, zt_send, zt_recv,
     one_send, one_recv, two_send, two_recv,
 ):
@@ -83,6 +104,7 @@
         pltpu.make_async_copy(base_ref, base_v, local_sem.at[2]),
         pltpu.make_async_copy(par_ref, par_v, local_sem.at[3]),
         pltpu.make_async_copy(latz_ref, latz_v, local_sem.at[4]),
+        pltpu.make_async_copy(trz_ref, trz_s, local_sem.at[5]),
     ]
     for copy in copies:
         copy.start()
@@ -93,8 +115,8 @@
     qcol[...] = jnp.broadcast_to(base_v[1:2, :], (LANES, LANES)).T
     row8 = lax.broadcasted_iota(jnp.int32, (8, LANES), 0)
     upper = row8 < 4
-    z_real = trz_ref[0]
-    z_imag = trz_ref[1]
+    z_real = trz_s[0]
+    z_imag = trz_s[1]
     zsec[ss, 0] = jnp.zeros((8, LANES), F32) + z_real
     zsec[ss, 1] = jnp.where(upper, -z_imag, z_imag)
 
@@ -217,11 +239,6 @@
                 cur[c, 0:2 * LANES, :], wlast[4 * LANES:6 * LANES, :], ((0,), (0,))
             )
 
-    def sweep(k, c):
-        currents(k, c, heads(k - 1, c) if k else None)
-        send_one(k, c)
-        products(k, c)
-
     def finish(c):
         head = heads(SWEEPS - 1, c).T
         at = lax.rem(node + offsets[c], nodes) * chunk
@@ -247,119 +264,115 @@
             device_id={"feeder": partner, "node": node}, device_id_type=MESH,
         )
 
-    level(0)
-    currents(0, 0, None)
-    pl.semaphore_wait(barrier, greeted)
-    for d in wide_turns:
-        pltpu.make_async_remote_copy(
-            src_ref=zsec.at[ss], dst_ref=zsec.at[ss], send_sem=zs_send, recv_sem=zs_recv,
-            device_id=at_slab(slab_mate(d)), device_id_type=MESH,
-        ).start()
-    send_one(0, 0)
-    for c in range(1, nodes):
-        give(c).start()
-
-    width = LANES
-    down = lax.broadcasted_iota(jnp.int32, (width, width), 0)
-    across = lax.broadcasted_iota(jnp.int32, (width, width), 1)
-    adjacent = jnp.where(jnp.broadcast_to(par_v[...], (width, width)) == down, 1.0, 0.0).T
-    paths = jnp.where(down == across, 1.0, 0.0) + adjacent
-    power = adjacent.astype(BF16)
-    for turn_ in range((width - 1).bit_length() - 1):
-        power = dot(power, power).astype(BF16)
-        paths = paths + dot(paths.astype(BF16), power)
-    paths_low = paths.astype(BF16)
-    for part in range(2):
-        z_row = jnp.broadcast_to(latz_v[part:part + 1, :], (width, width))
-        z_high, z_mid = halves(z_row)
-        z_low = (z_row - z_high.astype(F32) - z_mid.astype(F32)).astype(BF16)
-        table = jnp.zeros((width, width), F32)
-        for piece in (z_low, z_mid, z_high):
-            table += dot((paths * piece.astype(F32)).astype(BF16), paths_low, ((1,), (1,)))
-        prep[part] = table
-    for part, sign, r0, c0 in ((0, 1.0, 0, 0), (1, -1.0, 0, 1), (1, 1.0, 1, 0), (0, 1.0, 1, 1)):
-        high, low = halves(prep[part] * sign)
-        rs, cs = slice(r0 * width, (r0 + 1) * width), slice(c0 * width, (c0 + 1) * width)
-        wide[rs, cs] = high
-        wide[rs, (c0 + 2) * width:(c0 + 3) * width] = high
-        wlow[rs, cs] = low
-        ts, us = slice(c0 * width, (c0 + 1) * width), slice(r0 * width, (r0 + 1) * width)
-        wlast[ts, us] = high
-        wlast[(c0 + 2) * width:(c0 + 3) * width, us] = high
-        wlast[(c0 + 4) * width:(c0 + 5) * width, us] = low
-
-    wait_bytes(zs_recv, zsec.at[pl.ds(0, slab - 1)])
-    run_r = jnp.zeros((8, LANES), F32)
-    run_i = run_r
-    cut_r = run_r
-    cut_i = run_r
-    for s in range(slab):
-        run_r += zsec[s, 0]
-        run_i += zsec[s, 1]
-        cut_r += jnp.where(s <= ss, zsec[s, 0], 0.0)
-        cut_i += jnp.where(s <= ss, zsec[s, 1], 0.0)
-        zlow[s, 0] = run_r
-        zlow[s, 1] = run_i
-        zmin[s, 0] = cut_r
-        zmin[s, 1] = cut_i
-    ztot[zz, 0] = run_r
-    ztot[zz, 1] = run_i
-    for d in far:
-        pltpu.make_async_remote_copy(
-            src_ref=ztot.at[zz], dst_ref=ztot.at[zz], send_sem=zt_send, recv_sem=zt_recv,
-            device_id=at_other(lax.rem(zz + d, slabs)), device_id_type=MESH,
-        ).start()
-    combine(0, 0)
-    products(0, 0)
-
-    def bring(c):
-        give(c).wait_recv()
-        pass_on(c).start()
-
-    def begin(c):
-        pass_on(c).wait_recv()
-        level(c)
-        sweep(0, c)
-
-    bring(1)
-    if nodes > 2:
-        bring(2)
-    begin(1)
-    if nodes > 2:
-        begin(2)
-    combine(0, 1)
-    if nodes > 2:
-        combine(0, 2)
-    for c in range(3, nodes):
-        bring(c)
-        begin(c)
-
-    wait_bytes(zt_recv, ztot.at[pl.ds(0, slabs - 1)])
-    run_r = jnp.zeros((8, LANES), F32)
-    run_i = run_r
-    for z in range(slabs):
-        zpre[z, 0] = run_r
-        zpre[z, 1] = run_i
-        run_r += ztot[z, 0]
-        run_i += ztot[z, 1]
-
-    for k in range(1, SWEEPS + 1):
-        last = k == SWEEPS
-        step = finish if last else functools.partial(sweep, k)
-        step(0)
-        for c in range(3, nodes):
-            combine(k - 1, c)
-        if not last:
-            combine(k, 0)
-        step(1)
-        if nodes > 2:
-            step(2)
-        if not last:
-            combine(k, 1)
-            if nodes > 2:
-                combine(k, 2)
-        for c in range(3, nodes):
-            step(c)
+    def open_up():
+        pl.semaphore_wait(barrier, greeted)
+        for d in wide_turns:
+            pltpu.make_async_remote_copy(
+                src_ref=zsec.at[ss], dst_ref=zsec.at[ss], send_sem=zs_send, recv_sem=zs_recv,
+                device_id=at_slab(slab_mate(d)), device_id_type=MESH,
+            ).start()
+        send_one(0, 0)
+        for c in range(1, min(nodes, 3)):
+            give(c).start()
+
+    def tables():
+        width = LANES
+        down = lax.broadcasted_iota(jnp.int32, (width, width), 0)
+        across = lax.broadcasted_iota(jnp.int32, (width, width), 1)
+        adjacent = jnp.where(jnp.broadcast_to(par_v[...], (width, width)) == down, 1.0, 0.0).T
+        paths = jnp.where(down == across, 1.0, 0.0) + adjacent
+        power = adjacent.astype(BF16)
+        for turn_ in range((width - 1).bit_length() - 1):
+            power = dot(power, power).astype(BF16)
+            paths = paths + dot(paths.astype(BF16), power)
+        paths_low = paths.astype(BF16)
+        for part in range(2):
+            z_row = jnp.broadcast_to(latz_v[part:part + 1, :], (width, width))
+            z_high, z_mid = halves(z_row)
+            z_low = (z_row - z_high.astype(F32) - z_mid.astype(F32)).astype(BF16)
+            table = jnp.zeros((width, width), F32)
+            for piece in (z_low, z_mid, z_high):
+                table += dot((paths * piece.astype(F32)).astype(BF16), paths_low, ((1,), (1,)))
+            prep[part] = table
+        for part, sign, r0, c0 in ((0, 1.0, 0, 0), (1, -1.0, 0, 1), (1, 1.0, 1, 0), (0, 1.0, 1, 1)):
+            high, low = halves(prep[part] * sign)
+            rs, cs = slice(r0 * width, (r0 + 1) * width), slice(c0 * width, (c0 + 1) * width)
+            wide[rs, cs] = high
+            wide[rs, (c0 + 2) * width:(c0 + 3) * width] = high
+            wlow[rs, cs] = low
+            ts, us = slice(c0 * width, (c0 + 1) * width), slice(r0 * width, (r0 + 1) * width)
+            wlast[ts, us] = high
+            wlast[(c0 + 2) * width:(c0 + 3) * width, us] = high
+            wlast[(c0 + 4) * width:(c0 + 5) * width, us] = low
+
+    def slab_z():
+        wait_bytes(zs_recv, zsec.at[pl.ds(0, slab - 1)])
+        run_r = jnp.zeros((8, LANES), F32)
+        run_i = run_r
+        cut_r = run_r
+        cut_i = run_r
+        for s in range(slab):
+            run_r += zsec[s, 0]
+            run_i += zsec[s, 1]
+            cut_r += jnp.where(s <= ss, zsec[s, 0], 0.0)
+            cut_i += jnp.where(s <= ss, zsec[s, 1], 0.0)
+            zlow[s, 0] = run_r
+            zlow[s, 1] = run_i
+            zmin[s, 0] = cut_r
+            zmin[s, 1] = cut_i
+        ztot[zz, 0] = run_r
+        ztot[zz, 1] = run_i
+        for d in far:
+            pltpu.make_async_remote_copy(
+                src_ref=ztot.at[zz], dst_ref=ztot.at[zz], send_sem=zt_send, recv_sem=zt_recv,
+                device_id=at_other(lax.rem(zz + d, slabs)), device_id_type=MESH,
+            ).start()
+    def trunk_z():
+        wait_bytes(zt_recv, ztot.at[pl.ds(0, slabs - 1)])
+        run_r = jnp.zeros((8, LANES), F32)
+        run_i = run_r
+        for z in range(slabs):
+            zpre[z, 0] = run_r
+            zpre[z, 1] = run_i
+            run_r += ztot[z, 0]
+            run_i += ztot[z, 1]
+
+    def do(name):
+        if name == "P":
+            tables()
+            for c in range(3, nodes):
+                give(c).start()
+        elif name == "S":
+            slab_z()
+        elif name == "Z":
+            trunk_z()
+        elif name == "X":
+            open_up()
+        elif name[0] == "G":
+            give(int(name[1])).wait_recv()
+            pass_on(int(name[1])).start()
+        elif name[0] == "L":
+            c = int(name[1])
+            if c:
+                pass_on(c).wait_recv()
+            level(c)
+        elif name[0] == "F":
+            finish(int(name[1]))
+        else:
+            k, c = int(name[1]), int(name[2])
+            if name[0] in "AC":
+                currents(k, c, heads(k - 1, c) if k else None)
+            if name[0] == "A":
+                send_one(k, c)
+            if name[0] == "M":
+                products(k, c)
+            if name[0] == "B":
+                combine(k, c)
+
+    for line in ORDER:
+        for name in line.split():
+            if int(name[-1] if name[-1].isdigit() else 0) < nodes:
+                do(name)
 
     wait_bytes(zs_send, zsec.at[pl.ds(0, slab - 1)])
     wait_bytes(zt_send, ztot.at[pl.ds(0, slabs - 1)])
@@ -372,18 +385,32 @@
             wait_bytes(two_send.at[k, c], tiles(k, c, slabs - 1))
 
 
+def store(in_r, in_i, out_r, out_i, sem):
+    rows = in_r.shape[0] // PIECES
+    copies = []
+    for p in range(PIECES):
+        where = pl.ds(p * rows, rows)
+        copies.append(pltpu.make_async_copy(in_r.at[where], out_r.at[where], sem.at[0, p]))
+        copies.append(pltpu.make_async_copy(in_i.at[where], out_i.at[where], sem.at[1, p]))
+    for copy in copies:
+        copy.start()
+    for copy in copies:
+        copy.wait()
+
+
 def local(slabs, slab, nodes, factors, loadings, parents, load_base, lateral_z, trunk_z):
     chunk, depth = factors.shape
     scen = chunk * nodes
     width = loadings.shape[0]
-    any_space = pl.BlockSpec(memory_space=pl.ANY)
+    any_space = pl.BlockSpec(memory_space=pltpu.HBM)
     dma = pltpu.SemaphoreType.DMA
+    hbm = functools.partial(pltpu.with_memory_space_constraint, memory_space=pltpu.HBM)
     out = jax.ShapeDtypeStruct((scen, width), F32)
     tile = (8, LANES)
-    return pl.pallas_call(
+    volts = pl.pallas_call(
         functools.partial(body, slabs, slab, nodes),
         out_shape=(out, out),
-        in_specs=[any_space] * 5 + [pl.BlockSpec(memory_space=pltpu.SMEM)],
+        in_specs=[any_space] * 6,
         out_specs=(pl.BlockSpec(memory_space=pltpu.VMEM),) * 2,
         scratch_shapes=[
             pltpu.VMEM((nodes, chunk, depth), BF16),
@@ -410,7 +437,8 @@
             pltpu.VMEM((1, width), jnp.int32),
             pltpu.VMEM((2, width), F32),
             pltpu.VMEM((2, width), F32),
-            dma((5,)),
+            pltpu.SMEM((2,), F32),
+            dma((6,)),
             dma((nodes,)),
             dma((nodes,)),
             dma((nodes,)),
@@ -427,7 +455,15 @@
         compiler_params=pltpu.CompilerParams(
             collective_id=0, has_side_effects=True, vmem_limit_bytes=48 * 1024 * 1024
         ),
-    )(factors, loadings, parents.reshape(1, width), load_base, lateral_z, trunk_z.reshape(2))
+    )(*[hbm(a) for a in (factors, loadings, parents.reshape(1, width), load_base, lateral_z, trunk_z.reshape(2))])
+    return pl.pallas_call(
+        store,
+        out_shape=(out, out),
+        in_specs=[pl.BlockSpec(memory_space=pltpu.VMEM)] * 2,
+        out_specs=(any_space,) * 2,
+        scratch_shapes=[dma((2, PIECES))],
+        compiler_params=pltpu.CompilerParams(vmem_limit_bytes=1024 * 1024),
+    )(*volts)
 
 
 def solution(mesh):

time: 54.8 us -> 46.9 us (0.86)
  local copies, waits for them, and re-layouts: 4.41 us -> 0 us
  Pallas kernels: 49.5 us -> 46.2 us
    pallas_call x1, Pallas kernels: 49.5 us -> 44.8 us  [local(): pl.pallas_call(functools.partial(body, slabs, slab, nodes), out_shape=(ou...]
    unnamed x14 -> x0, local copies, waits for them, and re-layouts: 4.41 us -> none
    pallas_call x0 -> x1, Pallas kernels: none -> 1.38 us  [local(): pl.pallas_call(store, out_shape=(out, out), in_specs=[pl.BlockSpec(memory...]
where the time goes in v2:
time: 46.9 us; the launch traced here: 46.8 us
  Pallas kernels  46.2 us (99%)
  between operations  0.64 us (1%)
    pallas_call x1, Pallas kernels, local(): pl.pallas_call(functools.partial(body, slabs, slab, nodes), out_shape=(ou...  44.8 us
    pallas_call x1, Pallas kernels, local(): pl.pallas_call(store, out_shape=(out, out), in_specs=[pl.BlockSpec(memory...  1.38 us

profile of v2, /device:TPU:1, one launch (start us, length us, event | category | flops | bytes accessed | tf_op | source)
XLA Modules:
  0.0 46.8 jit_solution(11982900862376621331)
XLA Ops:
  0.6 44.8 %shard_map.77 = (f32[2048,128]{1,0:T(8,128)S(1)}, f32[2048,128]{1,0:T(8,128)S(1)}) custom-call(bf16[512,256]{1,0:T(8,128)(2,1)} %fac_ref.1, bf16[128,256]{1,0:T(8,128)(2,1)} %load_ref.1, s32[1,128]{1,0:T(1,128)} %bitcast.2, f32[2,128]{1,0:T(2,128)} %base_ref.1, f32[2,128]{1,0:T(2,128)} %latz_ref.1, f32[2]{0:T(128)} %bitcast.3), custom_call_target="tpu_custom_call" | custom-call | tf_op jit(solution)/shard_map/pallas_call | solution.py:410
  45.4 1.4 %shard_map.78 = (f32[2048,128]{1,0:T(8,128)}, f32[2048,128]{1,0:T(8,128)}) custom-call(f32[2048,128]{1,0:T(8,128)S(1)} %get-tuple-element.4.in_r, f32[2048,128]{1,0:T(8,128)S(1)} %get-tuple-element.5.in_i), custom_call_target="tpu_custom_call" | custom-call | tf_op jit(solution)/shard_map/pallas_call | solution.py:459

commit v3 on v2

--- a/solution.py
+++ b/solution.py
@@ -186,7 +186,7 @@
             total += tile
             weighted += zlow[s, 0] * tile + zlow[s, 1] * swapped
             own += zmin[s, 0] * tile + zmin[s, 1] * swapped
-        if k:
+        if k or c:
             shift = cmul((zpre[zz, 0], zpre[zz, 1]), total)
             weighted += shift
             own += shift
@@ -196,7 +196,7 @@
         two_own[k, c, 1] = own
         for d in far:
             other = lax.rem(zz + d, slabs)
-            if k:
+            if k or c:
                 later = (other > zz).astype(jnp.int32)
                 source = two_src.at[k, c, pl.ds(later, 1)]
                 target = two_sec.at[k, c, zz, pl.ds(0, 1)]
@@ -210,7 +210,7 @@
             ).start()
 
     def tiles(k, c, count):
-        if k:
+        if k or c:
             return two_sec.at[k, c, pl.ds(0, count), pl.ds(0, 1)]
         return two_sec.at[k, c, pl.ds(0, count)]
 
@@ -218,12 +218,12 @@
         wait_bytes(two_recv.at[k, c], tiles(k, c, slabs - 1))
         near = two_own[k, c, 1]
         beyond = jnp.zeros((8, LANES), F32)
-        if not k:
+        if not (k or c):
             near += cmul((zpre[zz, 0], zpre[zz, 1]), two_own[k, c, 0])
         for z in range(slabs):
             tile = two_sec[k, c, z, 0]
             beyond += jnp.where(z > zz, tile, 0.0)
-            if k:
+            if k or c:
                 near += jnp.where(z < zz, tile, 0.0)
             else:
                 given = cmul((zpre[z, 0], zpre[z, 1]), tile) + two_sec[k, c, z, 1]

time: 46.9 us -> 46.3 us (0.987)
  Pallas kernels: 46.2 us -> 45.5 us
    pallas_call x1, Pallas kernels: 44.8 us -> 44.2 us  [local(): pl.pallas_call(functools.partial(body, slabs, slab, nodes), out_shape=(ou...]
where the time goes in v3:
time: 46.3 us; the launch traced here: 46.2 us
  Pallas kernels  45.5 us (98%)
  between operations  0.64 us (1%)
    pallas_call x1, Pallas kernels, local(): pl.pallas_call(functools.partial(body, slabs, slab, nodes), out_shape=(ou...  44.2 us
    pallas_call x1, Pallas kernels, local(): pl.pallas_call(store, out_shape=(out, out), in_specs=[pl.BlockSpec(memory...  1.38 us

profile of v3, /device:TPU:1, one launch (start us, length us, event | category | flops | bytes accessed | tf_op | source)
XLA Modules:
  0.0 46.2 jit_solution(10983518378786861210)
XLA Ops:
  0.6 44.2 %shard_map.77 = (f32[2048,128]{1,0:T(8,128)S(1)}, f32[2048,128]{1,0:T(8,128)S(1)}) custom-call(bf16[512,256]{1,0:T(8,128)(2,1)} %fac_ref.1, bf16[128,256]{1,0:T(8,128)(2,1)} %load_ref.1, s32[1,128]{1,0:T(1,128)} %bitcast.2, f32[2,128]{1,0:T(2,128)} %base_ref.1, f32[2,128]{1,0:T(2,128)} %latz_ref.1, f32[2]{0:T(128)} %bitcast.3), custom_call_target="tpu_custom_call" | custom-call | tf_op jit(solution)/shard_map/pallas_call | solution.py:410
  44.8 1.4 %shard_map.78 = (f32[2048,128]{1,0:T(8,128)}, f32[2048,128]{1,0:T(8,128)}) custom-call(f32[2048,128]{1,0:T(8,128)S(1)} %get-tuple-element.4.in_r, f32[2048,128]{1,0:T(8,128)S(1)} %get-tuple-element.5.in_i), custom_call_target="tpu_custom_call" | custom-call | tf_op jit(solution)/shard_map/pallas_call | solution.py:459

commit v4 on v3

--- a/solution.py
+++ b/solution.py
@@ -159,7 +159,7 @@
                 )
 
             zero = jnp.zeros((8, LANES), F32)
-            sum_r, sum_i = lax.fori_loop(0, LANES // rows, step, (zero, zero), unroll=4)
+            sum_r, sum_i = lax.fori_loop(0, LANES // rows, step, (zero, zero), unroll=8)
             one_sec[k, c, ss, q:q + 1, :] = jnp.sum(sum_r, axis=0, keepdims=True)
             one_sec[k, c, ss, q + 4:q + 5, :] = jnp.sum(sum_i, axis=0, keepdims=True)
 

time: 46.3 us -> 46 us (level)
  no operation moved by 1% of the time
where the time goes in v4:
time: 46 us; the launch traced here: 45.9 us
  Pallas kernels  45.3 us (98%)
  between operations  0.64 us (1%)
    pallas_call x1, Pallas kernels, local(): pl.pallas_call(functools.partial(body, slabs, slab, nodes), out_shape=(ou...  43.9 us
    pallas_call x1, Pallas kernels, local(): pl.pallas_call(store, out_shape=(out, out), in_specs=[pl.BlockSpec(memory...  1.38 us

profile of v4, /device:TPU:1, one launch (start us, length us, event | category | flops | bytes accessed | tf_op | source)
XLA Modules:
  0.0 45.9 jit_solution(3251346828476367611)
XLA Ops:
  0.6 43.9 %shard_map.77 = (f32[2048,128]{1,0:T(8,128)S(1)}, f32[2048,128]{1,0:T(8,128)S(1)}) custom-call(bf16[512,256]{1,0:T(8,128)(2,1)} %fac_ref.1, bf16[128,256]{1,0:T(8,128)(2,1)} %load_ref.1, s32[1,128]{1,0:T(1,128)} %bitcast.2, f32[2,128]{1,0:T(2,128)} %base_ref.1, f32[2,128]{1,0:T(2,128)} %latz_ref.1, f32[2]{0:T(128)} %bitcast.3), custom_call_target="tpu_custom_call" | custom-call | tf_op jit(solution)/shard_map/pallas_call | solution.py:410
  44.5 1.4 %shard_map.78 = (f32[2048,128]{1,0:T(8,128)}, f32[2048,128]{1,0:T(8,128)}) custom-call(f32[2048,128]{1,0:T(8,128)S(1)} %get-tuple-element.4.in_r, f32[2048,128]{1,0:T(8,128)S(1)} %get-tuple-element.5.in_i), custom_call_target="tpu_custom_call" | custom-call | tf_op jit(solution)/shard_map/pallas_call | solution.py:459
